TPU v7x, 512 devices: a whole 4x8x8 slice. The times are simulated.
512 devices in a mesh: expert: 64 (over z, y), tensor: 8 (over x, core).
Axes of the slice: x: 4, y: 8, z: 8, core: 2. Of those that a mesh axis runs over, the one named last changes fastest.
Arguments:
- attn_out: bfloat16 [8192, 4096], P('expert', 'tensor'), may hold values from -6 to 6
- out_weight: bfloat16 [4096, 2048], P('tensor'), may hold values from -0.09375 to 0.09375
- residual: bfloat16 [8192, 2048], P(('expert', 'tensor')), may hold values from -6 to 6
- attn_gain: float32 [2048], replicated, may hold values from 0.1 to 1.9
- expert_ids: int32 [8192, 8], P('expert'), may hold values from 0 to 127, all different within a row; in each aligned block of 128 rows (0 to 127, 128 to 255, ...) at most 12 rows name the same one
- route_weights: float32 [8192, 8], P('expert'), may hold values from 0.05 to 0.3
- w_gate: bfloat16 [64, 2048, 1536], P('expert', None, 'tensor'), may hold values from -0.125 to 0.125
- w_up: bfloat16 [64, 2048, 1536], P('expert', None, 'tensor'), may hold values from -0.125 to 0.125
- w_down: bfloat16 [64, 1536, 2048], P('expert', 'tensor'), may hold values from -0.21875 to 0.21875
- input_gain: float32 [2048], replicated, may hold values from 0.1 to 1.9
- q_weight: bfloat16 [2048, 4096], P('expert', 'tensor'), may hold values from -0.125 to 0.125
- kv_weight: bfloat16 [2048, 1024], P('expert', 'tensor'), may hold values from -0.125 to 0.125
- q_gain: float32 [128], replicated, may hold values from 0.1 to 1.9
- k_gain: float32 [128], replicated, may hold values from 0.1 to 1.9
Outputs:
- next_residual: bfloat16 [8192, 2048], P(('expert', 'tensor'))
- queries: bfloat16 [8192, 4096], P('expert', 'tensor')
- keys_values: bfloat16 [8192, 1024], P('expert', 'tensor')
Inputs may be any that keep to these rules, and one draw needn't show every extreme that they name: `expert_ids`: each row names 8 different experts. In each aligned block of 128 rows no expert is named by more than 12 rows, and in some block one expert is named by exactly 12 rows.
All inputs are finite; a program needn't handle non-finite values.
Results may differ from a plain program's by a relative error of at most 0.012.
Values may be sent and summed in bfloat16 or wider, within the bound.
A program may use at most 64 MiB of HBM per device.

v0:
```python
import jax
import jax.numpy as jnp
from jax import lax
from jax.sharding import PartitionSpec as P

KV_HEADS = 4
TOP = 8
EPSILON = 1e-06


def normalize(values, gain):
    return values * lax.rsqrt(jnp.mean(values * values, axis=-1, keepdims=True) + EPSILON) * gain


def per_device(
    attn_out,
    out_weight,
    residual,
    attn_gain,
    expert_ids,
    route_weights,
    w_gate,
    w_up,
    w_down,
    input_gain,
    q_weight,
    kv_weight,
    q_gain,
    k_gain,
):
    n_expert = lax.axis_size("expert")
    n_tensor = lax.axis_size("tensor")
    share = n_tensor // 2
    tensor_index = lax.axis_index("tensor")
    group_rows = attn_out.shape[0]
    width = residual.shape[1]
    half = tensor_index // share
    capacity = 3 * group_rows * TOP // (4 * n_expert)
    all_experts = 2 * n_expert
    attn_rows = lax.psum_scatter(
        jnp.dot(attn_out, out_weight, preferred_element_type=jnp.float32),
        "tensor",
        scatter_dimension=0,
        tiled=True,
    )
    first_residual = (residual.astype(jnp.float32) + attn_rows).astype(jnp.bfloat16)
    normed = normalize(first_residual.astype(jnp.float32), attn_gain).astype(jnp.bfloat16)
    group_normed = lax.all_gather(normed, "tensor", axis=0, tiled=True)
    flat_ids = expert_ids.reshape(-1)
    onehot = (flat_ids[:, None] == jnp.arange(all_experts, dtype=jnp.int32)[None, :]).astype(
        jnp.int32
    )
    earlier = jnp.cumsum(onehot, axis=0) - onehot
    rank = jnp.sum(earlier * onehot, axis=1)
    dest = flat_ids * capacity + rank
    row_owner = jnp.arange(flat_ids.shape[0], dtype=jnp.int32) // TOP
    slot_row = jnp.full((all_experts * capacity,), group_rows, jnp.int32).at[dest].set(row_owner)
    slot_weight = (
        jnp.zeros((all_experts * capacity,), jnp.float32).at[dest].set(route_weights.reshape(-1))
    )
    own_slots = lax.dynamic_index_in_dim(
        slot_row.reshape(n_expert, 2, capacity), half, 1, keepdims=False
    )
    own_weights = lax.dynamic_index_in_dim(
        slot_weight.reshape(n_expert, 2, capacity), half, 1, keepdims=False
    )
    padded_rows = jnp.concatenate([group_normed, jnp.zeros((1, width), jnp.bfloat16)], axis=0)
    gate_w = w_gate[0]
    up_w = w_up[0]
    down_w = w_down[0]
    outgoing = jnp.take(padded_rows, own_slots, axis=0)
    arrived = lax.all_to_all(outgoing, "expert", split_axis=0, concat_axis=0, tiled=True)
    flat = arrived.reshape(-1, width)
    gate = jnp.dot(flat, gate_w, preferred_element_type=jnp.float32)
    up = jnp.dot(flat, up_w, preferred_element_type=jnp.float32)
    act = (jax.nn.silu(gate) * up).astype(jnp.bfloat16)
    part = jnp.dot(act, down_w, preferred_element_type=jnp.float32).astype(jnp.bfloat16)
    send_part = part.reshape(arrived.shape)
    returned = lax.all_to_all(send_part, "expert", split_axis=0, concat_axis=0, tiled=True)
    weighted = own_weights.reshape(-1)[:, None] * returned.reshape(-1, width).astype(jnp.float32)
    term = (
        jnp.zeros((group_rows + 1, width), jnp.float32)
        .at[own_slots.reshape(-1)]
        .add(weighted)[:group_rows]
    )
    expert_sum = lax.psum_scatter(
        term.astype(jnp.bfloat16), "tensor", scatter_dimension=0, tiled=True
    ).astype(jnp.float32)
    next_residual = (first_residual.astype(jnp.float32) + expert_sum).astype(jnp.bfloat16)
    own_normed = normalize(next_residual.astype(jnp.float32), input_gain).astype(jnp.bfloat16)
    next_normed = lax.all_gather(own_normed, "tensor", axis=0, tiled=True)
    query_cols = q_weight.shape[1]
    kv_cols = kv_weight.shape[1]
    query_raw = jnp.dot(
        next_normed,
        lax.all_gather(q_weight, "expert", axis=0, tiled=True),
        preferred_element_type=jnp.float32,
    )
    kv_raw = jnp.dot(
        next_normed,
        lax.all_gather(kv_weight, "expert", axis=0, tiled=True),
        preferred_element_type=jnp.float32,
    )
    head_size = q_gain.shape[0]
    queries = (
        normalize(query_raw.reshape(group_rows, -1, head_size), q_gain)
        .reshape(group_rows, query_cols)
        .astype(jnp.bfloat16)
    )
    heads_here = kv_cols // head_size
    head_number = tensor_index * heads_here + jnp.arange(heads_here, dtype=jnp.int32)
    is_key = head_number < KV_HEADS
    kv_shaped = kv_raw.reshape(group_rows, heads_here, head_size)
    keys_values = (
        jnp.where(is_key[None, :, None], normalize(kv_shaped, k_gain), kv_shaped)
        .reshape(group_rows, kv_cols)
        .astype(jnp.bfloat16)
    )
    return (next_residual, queries, keys_values)


def solution(mesh):
    return jax.shard_map(
        per_device,
        mesh=mesh,
        in_specs=(
            P("expert", "tensor"),
            P("tensor", None),
            P(("expert", "tensor"), None),
            P(),
            P("expert", None),
            P("expert", None),
            P("expert", None, "tensor"),
            P("expert", None, "tensor"),
            P("expert", "tensor", None),
            P(),
            P("expert", "tensor"),
            P("expert", "tensor"),
            P(),
            P(),
        ),
        out_specs=(P(("expert", "tensor"), None), P("expert", "tensor"), P("expert", "tensor")),
        check_vma=False,
    )
```

profile of v0, /device:TPU:2, one launch (start us, length us, event | category | flops | bytes accessed | tf_op | source)
XLA Modules:
  0.0 475.3 jit_solution(3789116620057749564)
XLA Ops:
  8.0 0.0 copy-start
  8.0 0.0 reduce-scatter.3.cloned.1.call-start
  8.1 1.5 copy-done
  9.6 2.3 fusion.42
  11.9 0.0 reduce-scatter.3.cloned.1.call-update
  12.0 0.1 copy.34
  12.1 0.1 eq.29
  12.2 0.1 eq.25
  12.3 0.1 copy.33
  12.4 0.1 mul.128
  12.5 0.1 copy.36
  12.6 0.2 fusion.17
  12.9 0.1 copy.37
  13.0 0.4 fusion.16
  13.4 4.3 scatter_custom_fusion
  17.7 0.1 reshape.200
  17.9 0.5 broadcast.190
  18.4 0.7 fusion.40
  19.2 0.1 reshape.209
  19.3 32.0 %reduce-scatter.3.cloned.1.call-done = f32[16,2048]{1,0:T(8,128)} async-done(((f32[128,2048]{1,0:T(8,128)}), f32[16,2048]{1,0:T(8,128)}) %reduce-scatter.3.cloned.1.call-update) | async-done | bytes 131088 | tf_op jit(solution)/shard_map/reduce_scatter | solution.py:40
  51.3 0.0 copy-done.2
  51.3 1.0 fusion.26
  52.3 0.1 fusion.28
  52.4 13.8 %all_gather.12 = bf16[128,2048]{1,0:T(8,128)(2,1)S(1)} all-gather(bf16[16,2048]{1,0:T(8,128)(2,1)S(1)} %fusion.28), channel_id=1, replica_groups=mesh['expert'=64,'tensor'=8] {'tensor'}, dimensions={0}, use_global_device_ids=true | all-gather | bytes 589824 | tf_op jit(solution)/shard_map/all_gather | solution.py:48
  66.3 4.3 gather_fusion
  70.6 6.1 %reshape.208 = bf16[64,12,2048]{2,1,0:T(8,128)(2,1)} reshape(bf16[768,2048]{1,0:T(8,128)(2,1)} %gather_fusion) | data formatting | bytes 6291456 | tf_op jit(solution)/shard_map/jit(_take)/gather | solution.py:71
  76.6 2.6 broadcast_select_fusion
  79.3 111.8 %all_to_all.10 = bf16[64,12,2048]{2,1,0:T(8,128)(2,1)} all-to-all(bf16[64,12,2048]{2,1,0:T(8,128)(2,1)S(1)} %broadcast_select_fusion), channel_id=1, replica_groups=mesh['expert'=64,'tensor'=8] {'expert'}, dimensions={0} | all-to-all | bytes 6291456 | tf_op jit(solution)/shard_map/all_to_all | solution.py:72
  191.1 6.2 %reshape.204 = bf16[768,2048]{1,0:T(8,128)(2,1)} reshape(bf16[64,12,2048]{2,1,0:T(8,128)(2,1)} %all_to_all.10) | data formatting | bytes 6291456 | tf_op jit(solution)/shard_map/reshape | solution.py:73
  197.3 3.3 fusion.7
  200.5 6.5 %convolution_convert_fusion = bf16[768,2048]{1,0:T(8,128)(2,1)} fusion(bf16[768,2048]{1,0:T(8,128)(2,1)} %reshape.204, bf16[1,192,2048]{2,1,0:T(8,128)(2,1)} %param.22, bf16[1,2048,192]{1,2,0:T(8,128)(2,1)} %param.21, f32[768,192]{0,1:T(8,128)S(1)} %fusion.7), kind=kOutput, calls=%fused_computation.7 | convolution fusion | flops 1210417152 | bytes 8454144 | tf_op jit(solution)/shard_map/dot_general | solution.py:77
  207.0 6.1 %reshape.205 = bf16[64,12,2048]{2,1,0:T(8,128)(2,1)} reshape(bf16[768,2048]{1,0:T(8,128)(2,1)} %convolution_convert_fusion) | data formatting | bytes 6291456 | tf_op jit(solution)/shard_map/reshape | solution.py:78
  213.1 12.7 %all-to-all-start.1 = ((bf16[64,12,2048]{2,1,0:T(8,128)(2,1)}), bf16[64,12,2048]{2,1,0:T(8,128)(2,1)}, u32[]{:S(2)}, u32[]{:S(2)}) async-start(bf16[64,12,2048]{2,1,0:T(8,128)(2,1)} %reshape.205), calls=%async_computation.2 | async-start | bytes 8388608 | tf_op jit(solution)/shard_map/all_to_all | solution.py:79
  225.8 0.0 reduce-scatter.5.cloned.1.call-start
  225.9 0.1 reshape.201
  226.0 0.1 copy.38
  226.1 0.1 reshape.227
  226.2 4.5 scatter_custom_fusion.1
  230.7 0.1 reshape.203
  230.9 0.1 dynamic-slice_reduce_fusion
  231.0 0.1 mul.130
  231.1 96.7 %all-to-all-done.1 = bf16[64,12,2048]{2,1,0:T(8,128)(2,1)} async-done(((bf16[64,12,2048]{2,1,0:T(8,128)(2,1)}), bf16[64,12,2048]{2,1,0:T(8,128)(2,1)}, u32[]{:S(2)}, u32[]{:S(2)}) %all-to-all-start.1) | async-done | bytes 3145760 | tf_op jit(solution)/shard_map/all_to_all | solution.py:79
  327.8 6.7 %reshape.206 = f32[768,2048]{1,0:T(8,128)} reshape(bf16[64,12,2048]{2,1,0:T(8,128)(2,1)} %all-to-all-done.1) | data formatting | bytes 9437184 | tf_op jit(solution)/shard_map/convert_element_type | solution.py:80
  334.5 15.8 %scatter_custom_fusion.2 = f32[129,2048]{1,0:T(8,128)S(1)} fusion(s32[768]{0:T(1024)S(1)} %fusion.37, f32[768,2048]{1,0:T(8,128)} %reshape.206, f32[768]{0:T(1024)S(1)} %mul.130, f32[]{:T(128)} %constant.76.clone.1), kind=kCustom, calls=%fused_computation.4 | custom fusion | flops 3145728 | bytes 7352324 | tf_op jit(solution)/shard_map/scatter-add | solution.py:84
  350.3 0.9 slice.20
  351.1 0.0 reduce-scatter.5.cloned.1.call-update
  351.1 0.0 all-gather.2.cloned.1.call-start
  351.2 0.5 all-gather.2.cloned.1.call-update
  351.7 72.7 %all_gather.15 = bf16[2048,128]{1,0:T(8,128)(2,1)S(1)} all-gather(bf16[32,128]{1,0:T(8,128)(2,1)S(1)} %copy-done.4), channel_id=1, replica_groups=mesh['expert'=64,'tensor'=8] {'expert'}, dimensions={0}, use_global_device_ids=true | all-gather | bytes 532480 | tf_op jit(solution)/shard_map/all_gather | solution.py:101
  424.5 0.0 copy-start.8
  424.5 0.0 reduce-scatter.5.cloned.1.call-done
  424.5 1.0 fusion.23
  425.5 0.1 fusion.25
  425.6 13.1 %all_gather.13 = bf16[128,2048]{1,0:T(8,128)(2,1)S(1)} all-gather(bf16[16,2048]{1,0:T(8,128)(2,1)S(1)} %fusion.25), channel_id=1, replica_groups=mesh['expert'=64,'tensor'=8] {'tensor'}, dimensions={0}, use_global_device_ids=true | all-gather | bytes 589824 | tf_op jit(solution)/shard_map/all_gather | solution.py:91
  438.7 19.9 %all-gather.2.cloned.1.call-done = bf16[2048,512]{1,0:T(8,128)(2,1)} async-done(((bf16[32,512]{1,0:T(8,128)(2,1)}), bf16[2048,512]{1,0:T(8,128)(2,1)}) %all-gather.2.cloned.1.call-update) | async-done | bytes 2097168 | tf_op jit(solution)/shard_map/all_gather | solution.py:96
  458.6 2.8 fusion.41
  461.4 1.7 mul.146
  463.1 1.8 reduce_sum.51
  464.9 0.9 add_rsqrt_fusion
  465.7 0.4 multiply_reduce_fusion
  466.1 0.1 select_convert_fusion
  466.2 0.7 copy.41
  466.9 0.2 mul.147
  467.1 0.7 fusion.21
  (32 shorter events, 0.2 us)
Async XLA Ops:
  8.0 1.6 copy-start
  8.0 4.0 copy-start.3
  8.0 43.2 %reduce-scatter.3.cloned.1.call-start = ((), (), s32[]{:S(2)}) async-start(), calls=%async_computation.4 | async-start | bytes 1179648 | tf_op jit(solution)/shard_map/reduce_scatter | solution.py:40
  11.9 39.3 %copy-start.2 = (bf16[16,2048]{1,0:T(8,128)(2,1)S(1)}, bf16[16,2048]{1,0:T(8,128)(2,1)}, u32[]{:S(2)}) copy-start(bf16[16,2048]{1,0:T(8,128)(2,1)} %param.16) | copy-start | bytes 196612
  11.9 40.4 %copy-start.5 = (f32[2048]{0:T(1024)S(1)}, f32[2048]{0:T(1024)}, u32[]{:S(2)}) copy-start(f32[2048]{0:T(1024)} %param.17) | copy-start | bytes 24580
  213.1 12.9 %copy-start.7 = (f32[128,8]{0,1:T(8,128)S(1)}, f32[128,8]{0,1:T(8,128)}, u32[]{:S(2)}) copy-start(f32[128,8]{0,1:T(8,128)} %param.19) | copy-start | bytes 12292
  213.1 114.7 %all-to-all-start.1 = ((bf16[64,12,2048]{2,1,0:T(8,128)(2,1)}), bf16[64,12,2048]{2,1,0:T(8,128)(2,1)}, u32[]{:S(2)}, u32[]{:S(2)}) async-start(bf16[64,12,2048]{2,1,0:T(8,128)(2,1)} %reshape.205), calls=%async_computation.2 | async-start | bytes 8388608 | tf_op jit(solution)/shard_map/all_to_all | solution.py:79
  225.8 198.7 %reduce-scatter.5.cloned.1.call-start = ((), (), s32[]{:S(2)}) async-start(), calls=%async_computation.5 | async-start | bytes 589824 | tf_op jit(solution)/shard_map/reduce_scatter | solution.py:86
  334.5 17.3 %copy-start.4 = (bf16[32,128]{1,0:T(8,128)(2,1)S(1)}, bf16[32,128]{1,0:T(8,128)(2,1)}, u32[]{:S(2)}) copy-start(bf16[32,128]{1,0:T(8,128)(2,1)} %param.25) | copy-start | bytes 24580
  334.5 90.0 %copy-start.9 = (f32[128]{0:T(128)S(1)}, f32[128]{0:T(128)}, u32[]{:S(2)}) copy-start(f32[128]{0:T(128)} %param.26) | copy-start | bytes 1540
  334.5 91.0 %copy-start.6 = (f32[2048]{0:T(1024)S(1)}, f32[2048]{0:T(1024)}, u32[]{:S(2)}) copy-start(f32[2048]{0:T(1024)} %param.23) | copy-start | bytes 24580
  351.1 107.4 %all-gather.2.cloned.1.call-start = ((), (), s32[]{:S(2)}) async-start(), calls=%async_computation.6 | async-start | bytes 2129920 | tf_op jit(solution)/shard_map/all_gather | solution.py:96
  424.5 41.6 %copy-start.8 = (f32[128]{0:T(128)S(1)}, f32[128]{0:T(128)}, u32[]{:S(2)}) copy-start(f32[128]{0:T(128)} %param.27) | copy-start | bytes 1540
  425.5 41.6 %copy-start.1 = (bf16[16,2048]{1,0:T(8,128)(2,1)}, bf16[16,2048]{1,0:T(8,128)(2,1)S(1)}, u32[]{:S(2)}) copy-start(bf16[16,2048]{1,0:T(8,128)(2,1)S(1)} %get-tuple-element.16) | copy-start | bytes 196612
Sparse Core Ops, SparseCore 0:
  12.1 39.1 reduce-scatter.2
  351.3 53.9 reduce-scatter.4
Sparse Core Ops, SparseCore 1:
  354.7 103.8 all-gather.1
where the time goes:
time: 476 us; the launch traced here: 475 us
  blocking collectives  211 us (44%)
  waiting for transfers between devices  149 us (31%)
  local copies, waits for them, and re-layouts  46 us (10%)
  other arithmetic  24.7 us (5%)
  between operations  15.8 us (3%)
  matrix products  15.2 us (3%)
  starting transfers between devices  12.9 us (3%)
    all_to_all x1, blocking collectives, per_device(): lax.all_to_all(outgoing, 'expert', split_axis=0, concat_axis=0, tiled=True)  112 us
    all_to_all x1, waiting for transfers between devices, per_device(): lax.all_to_all(send_part, 'expert', split_axis=0, concat_axis=0, tiled=True)  96.7 us
    all_gather x1, blocking collectives, per_device(): lax.all_gather(kv_weight, 'expert', axis=0, tiled=True)  72.7 us
    reduce_scatter x1, waiting for transfers between devices, per_device(): lax.psum_scatter(jnp.dot(attn_out, out_weight, preferred_element_type=jnp...  32 us
    all_gather x1, waiting for transfers between devices, per_device(): lax.all_gather(q_weight, 'expert', axis=0, tiled=True)  19.9 us
    scatter-add x1, other arithmetic, per_device(): term = jnp.zeros((group_rows + 1, width), jnp.float32).at[own_slots.resha...  15.8 us
    all_gather x1, blocking collectives, per_device(): group_normed = lax.all_gather(normed, 'tensor', axis=0, tiled=True)  13.8 us
    all_gather x1, blocking collectives, per_device(): next_normed = lax.all_gather(own_normed, 'tensor', axis=0, tiled=True)  13.1 us
  transfers between devices with their start and end apart: 4, of which 3 were waited for; matrix products, arithmetic and copies ran while one was open for 3% of the time, Pallas kernels for 0%

commit v1 on v0

--- a/solution.py
+++ b/solution.py
@@ -6,6 +6,14 @@
 KV_HEADS = 4
 TOP = 8
 EPSILON = 1e-06
+
+
+def floor_cut(local, row_dim):
+    local = jnp.moveaxis(local, 0, row_dim)
+    x_new = local.shape
+    return local.reshape(
+        *x_new[:row_dim], x_new[row_dim] * x_new[row_dim + 1], *x_new[row_dim + 2 :]
+    )
 
 
 def normalize(values, gain):
@@ -45,7 +53,29 @@
     )
     first_residual = (residual.astype(jnp.float32) + attn_rows).astype(jnp.bfloat16)
     normed = normalize(first_residual.astype(jnp.float32), attn_gain).astype(jnp.bfloat16)
-    group_normed = lax.all_gather(normed, "tensor", axis=0, tiled=True)
+    lanes = lax.axis_size("tensor")
+    gallery = []
+    for b in tuple(range(lanes)):
+        gallery.append((b, (b + 1) % lanes))
+    buffers = []
+    for u, to_i in gallery:
+        buffers.append((to_i, u))
+    z2, part_now = ([], [])
+    for dev_i in [*range(lanes - 1)]:
+        if dev_i % 2 == 0:
+            even = lax.ppermute(z2[-1] if z2 else normed, axis_name="tensor", perm=gallery)
+            z2.append(even)
+        else:
+            small = lax.ppermute(
+                part_now[-1] if part_now else normed, axis_name="tensor", perm=buffers
+            )
+            part_now.append(small)
+    moved = jnp.stack([*z2[::-1], normed, *part_now], 0)
+    taken_in = lax.axis_index("tensor")
+    all_values = len(z2)
+    tall = taken_in - all_values
+    moved = moved[(jnp.arange(lanes) - tall) % lanes]
+    group_normed = floor_cut(moved, 0)
     flat_ids = expert_ids.reshape(-1)
     onehot = (flat_ids[:, None] == jnp.arange(all_experts, dtype=jnp.int32)[None, :]).astype(
         jnp.int32

time: 476 us -> 493 us (1.036)
  waiting for transfers between devices: 149 us -> 165 us
    all_gather x1, blocking collectives: 13.1 us -> 29.9 us  [per_device(): next_normed = lax.all_gather(own_normed, 'tensor', axis=0, tiled=True)]
    all_gather x1 -> x0, blocking collectives: 13.8 us -> none  [per_device(): group_normed = lax.all_gather(normed, 'tensor', axis=0, tiled=True)]
    ppermute x0 -> x7, waiting for transfers between devices: none -> 9.13 us  [the longest x4 9 us: per_device(): lax.ppermute(z2[-1] if z2 else normed, axis_name='tensor', perm=gallery)]
    ppermute x0 -> x7, starting transfers between devices: none -> 6.87 us  [the longest x3 6.85 us: per_device(): lax.ppermute(part_now[-1] if part_now else normed, axis_name='tensor', pe...]
    all_gather x1, blocking collectives: 72.7 us -> 67.6 us  [per_device(): lax.all_gather(kv_weight, 'expert', axis=0, tiled=True)]
  transfers between devices with their start and end apart: 4 -> 11, of which waited for: 3 -> 9; matrix products, arithmetic and copies ran while one was open for 3% -> 3% of each run, Pallas kernels for 0% -> 0%
where the time goes in v1:
time: 493 us; the launch traced here: 492 us
  blocking collectives  207 us (42%)
  waiting for transfers between devices  165 us (33%)
  local copies, waits for them, and re-layouts  46.7 us (9%)
  other arithmetic  24.8 us (5%)
  starting transfers between devices  16.2 us (3%)
  matrix products  16 us (3%)
  between operations  15.9 us (3%)
    all_to_all x1, blocking collectives, per_device(): lax.all_to_all(outgoing, 'expert', split_axis=0, concat_axis=0, tiled=True)  110 us
    all_to_all x1, waiting for transfers between devices, per_device(): lax.all_to_all(send_part, 'expert', split_axis=0, concat_axis=0, tiled=True)  99.4 us
    all_gather x1, blocking collectives, per_device(): lax.all_gather(kv_weight, 'expert', axis=0, tiled=True)  67.6 us
    reduce_scatter x1, waiting for transfers between devices, per_device(): lax.psum_scatter(jnp.dot(attn_out, out_weight, preferred_element_type=jnp...  32.1 us
    all_gather x1, blocking collectives, per_device(): next_normed = lax.all_gather(own_normed, 'tensor', axis=0, tiled=True)  29.9 us
    all_gather x1, waiting for transfers between devices, per_device(): lax.all_gather(q_weight, 'expert', axis=0, tiled=True)  21.8 us
    scatter-add x1, other arithmetic, per_device(): term = jnp.zeros((group_rows + 1, width), jnp.float32).at[own_slots.resha...  15.8 us
    gather x2, local copies, waits for them, and re-layouts, per_device(): outgoing = jnp.take(padded_rows, own_slots, axis=0)  10.3 us
  transfers between devices with their start and end apart: 11, of which 9 were waited for; matrix products, arithmetic and copies ran while one was open for 3% of the time, Pallas kernels for 0%

profile of v1, /device:TPU:2, one launch (start us, length us, event | category | flops | bytes accessed | tf_op | source)
XLA Modules:
  0.0 492.1 jit_solution(10050082329031320825)
XLA Ops:
  8.1 1.5 copy-done
  9.6 2.3 fusion.44
  12.0 0.1 copy.34
  12.1 0.1 eq.31
  12.2 0.1 eq.27
  12.3 0.1 copy.33
  12.4 0.1 mul.128
  12.5 0.1 copy.36
  12.6 0.2 fusion.17
  12.9 0.1 copy.37
  13.0 0.4 fusion.16
  13.4 4.3 scatter_custom_fusion
  17.7 0.1 reshape.252
  17.9 0.5 broadcast.259
  18.4 0.7 fusion.42
  19.2 32.1 %reduce-scatter.3.cloned.1.call-done = f32[16,2048]{1,0:T(8,128)} async-done(((f32[128,2048]{1,0:T(8,128)}), f32[16,2048]{1,0:T(8,128)}) %reduce-scatter.3.cloned.1.call-update) | async-done | bytes 131088 | tf_op jit(solution)/shard_map/reduce_scatter | solution.py:48
  51.3 1.0 fusion.26
  52.3 0.1 fusion.28
  52.5 0.1 reshape.270
  52.6 3.6 collective-permute-done
  56.1 1.8 collective-permute-start.4
  57.9 1.9 collective-permute-done.1
  59.8 2.1 collective-permute-start.5
  61.9 1.8 collective-permute-done.2
  63.7 0.1 collective-permute-done.5
  63.8 3.0 collective-permute-start.6
  66.8 1.8 collective-permute-done.3
  68.6 0.1 bitcast_dynamic-update-slice_fusion.3
  68.8 0.6 gather_fusion
  69.4 4.3 gather_fusion.1
  73.7 6.1 %reshape.269 = bf16[64,12,2048]{2,1,0:T(8,128)(2,1)} reshape(bf16[768,2048]{1,0:T(8,128)(2,1)} %gather_fusion.1) | data formatting | bytes 6291456 | tf_op jit(solution)/shard_map/jit(_take)/gather | solution.py:101
  79.8 2.6 broadcast_select_fusion
  82.4 110.0 %all_to_all.10 = bf16[64,12,2048]{2,1,0:T(8,128)(2,1)} all-to-all(bf16[64,12,2048]{2,1,0:T(8,128)(2,1)S(1)} %broadcast_select_fusion), channel_id=1, replica_groups=mesh['expert'=64,'tensor'=8] {'expert'}, dimensions={0} | all-to-all | bytes 6291456 | tf_op jit(solution)/shard_map/all_to_all | solution.py:102
  192.4 6.2 %reshape.257 = bf16[768,2048]{1,0:T(8,128)(2,1)} reshape(bf16[64,12,2048]{2,1,0:T(8,128)(2,1)} %all_to_all.10) | data formatting | bytes 6291456 | tf_op jit(solution)/shard_map/reshape | solution.py:103
  198.6 3.9 fusion.7
  202.5 6.7 %convolution_convert_fusion = bf16[768,2048]{1,0:T(8,128)(2,1)} fusion(bf16[768,2048]{1,0:T(8,128)(2,1)} %reshape.257, bf16[1,192,2048]{2,1,0:T(8,128)(2,1)} %param.22, bf16[1,2048,192]{1,2,0:T(8,128)(2,1)} %param.21, f32[768,192]{0,1:T(8,128)} %fusion.7), kind=kOutput, calls=%fused_computation.8 | convolution fusion | flops 1210417152 | bytes 8454144 | tf_op jit(solution)/shard_map/dot_general | solution.py:107
  209.2 6.1 %reshape.258 = bf16[64,12,2048]{2,1,0:T(8,128)(2,1)} reshape(bf16[768,2048]{1,0:T(8,128)(2,1)} %convolution_convert_fusion) | data formatting | bytes 6291456 | tf_op jit(solution)/shard_map/reshape | solution.py:108
  215.2 9.2 %all-to-all-start.1 = ((bf16[64,12,2048]{2,1,0:T(8,128)(2,1)}), bf16[64,12,2048]{2,1,0:T(8,128)(2,1)}, u32[]{:S(2)}, u32[]{:S(2)}) async-start(bf16[64,12,2048]{2,1,0:T(8,128)(2,1)} %reshape.258), calls=%async_computation.2 | async-start | bytes 8388608 | tf_op jit(solution)/shard_map/all_to_all | solution.py:109
  224.5 0.1 reshape.253
  224.6 0.1 copy.38
  224.8 0.1 reshape.288
  224.8 4.5 scatter_custom_fusion.1
  229.3 0.1 reshape.255
  229.5 0.1 dynamic-slice_reduce_fusion
  229.6 0.1 mul.130
  229.7 99.4 %all-to-all-done.1 = bf16[64,12,2048]{2,1,0:T(8,128)(2,1)} async-done(((bf16[64,12,2048]{2,1,0:T(8,128)(2,1)}), bf16[64,12,2048]{2,1,0:T(8,128)(2,1)}, u32[]{:S(2)}, u32[]{:S(2)}) %all-to-all-start.1) | async-done | bytes 3145760 | tf_op jit(solution)/shard_map/all_to_all | solution.py:109
  329.2 6.7 %reshape.259 = f32[768,2048]{1,0:T(8,128)} reshape(bf16[64,12,2048]{2,1,0:T(8,128)(2,1)} %all-to-all-done.1) | data formatting | bytes 9437184 | tf_op jit(solution)/shard_map/convert_element_type | solution.py:110
  335.8 15.8 %scatter_custom_fusion.2 = f32[129,2048]{1,0:T(8,128)S(1)} fusion(s32[768]{0:T(1024)S(1)} %fusion.37, f32[768,2048]{1,0:T(8,128)} %reshape.259, f32[768]{0:T(1024)S(1)} %mul.130, f32[]{:T(128)} %constant.90.clone.1), kind=kCustom, calls=%fused_computation.5 | custom fusion | flops 3145728 | bytes 7352324 | tf_op jit(solution)/shard_map/scatter-add | solution.py:114
  351.6 0.9 slice.22
  352.6 0.5 all-gather.2.cloned.1.call-update
  353.1 67.6 %all_gather.11 = bf16[2048,128]{1,0:T(8,128)(2,1)S(1)} all-gather(bf16[32,128]{1,0:T(8,128)(2,1)S(1)} %copy-done.5), channel_id=1, replica_groups=mesh['expert'=64,'tensor'=8] {'expert'}, dimensions={0}, use_global_device_ids=true | all-gather | bytes 532480 | tf_op jit(solution)/shard_map/all_gather | solution.py:131
  420.7 1.9 reduce-scatter.5.cloned.1.call-done
  422.6 1.0 fusion.23
  423.7 29.9 %all_gather.9 = bf16[128,2048]{1,0:T(8,128)(2,1)S(1)} all-gather(bf16[16,2048]{1,0:T(8,128)(2,1)S(1)} %fusion.25), channel_id=1, replica_groups=mesh['expert'=64,'tensor'=8] {'tensor'}, dimensions={0}, use_global_device_ids=true | all-gather | bytes 589824 | tf_op jit(solution)/shard_map/all_gather | solution.py:121
  453.6 21.8 %all-gather.2.cloned.1.call-done = bf16[2048,512]{1,0:T(8,128)(2,1)} async-done(((bf16[32,512]{1,0:T(8,128)(2,1)}), bf16[2048,512]{1,0:T(8,128)(2,1)}) %all-gather.2.cloned.1.call-update) | async-done | bytes 2097168 | tf_op jit(solution)/shard_map/all_gather | solution.py:126
  475.4 2.8 fusion.43
  478.2 1.7 mul.146
  479.9 1.8 reduce_sum.51
  481.7 0.9 add_rsqrt_fusion
  482.6 0.4 multiply_reduce_fusion
  482.9 0.1 select_convert_fusion
  483.0 0.7 copy.41
  483.8 0.2 mul.147
  484.0 0.7 fusion.21
  (58 shorter events, 0.6 us)
Async XLA Ops:
  8.0 1.6 copy-start
  8.0 4.0 copy-start.4
  8.0 43.2 %reduce-scatter.3.cloned.1.call-start = ((), (), s32[]{:S(2)}) async-start(), calls=%async_computation.4 | async-start | bytes 1179648 | tf_op jit(solution)/shard_map/reduce_scatter | solution.py:48
  11.9 39.3 %copy-start.2 = (bf16[16,2048]{1,0:T(8,128)(2,1)S(1)}, bf16[16,2048]{1,0:T(8,128)(2,1)}, u32[]{:S(2)}) copy-start(bf16[16,2048]{1,0:T(8,128)(2,1)} %param.16) | copy-start | bytes 196612
  11.9 40.4 %copy-start.3 = (f32[2048]{0:T(1024)S(1)}, f32[2048]{0:T(1024)}, u32[]{:S(2)}) copy-start(f32[2048]{0:T(1024)} %param.17) | copy-start | bytes 24580
  52.4 3.7 collective-permute-start
  56.1 3.7 collective-permute-start.1
  56.1 3.7 collective-permute-start.4
  59.8 3.9 collective-permute-start.2
  59.8 4.0 collective-permute-start.5
  63.7 4.9 collective-permute-start.3
  63.8 4.9 %collective-permute-start.6 = (bf16[16,2048]{1,0:T(8,128)(2,1)S(1)}, bf16[16,2048]{1,0:T(8,128)(2,1)S(1)}, u32[]{:S(2)}, u32[]{:S(2)}) collective-permute-start(bf16[16,2048]{1,0:T(8,128)(2,1)S(1)} %collective-permute-done.5), channel_id=1, source_target_pairs={{1,0},{2,1},{3,2},{4,3},{5,4},{6,5},{7,6},{0,7},{9,8},{10,9},{11,1... | collective-permute-start | bytes 196616 | tf_op jit(solution)/shard_map/ppermute | solution.py:69
  192.4 6.2 %copy-start.10 = (bf16[1,2048,192]{1,2,0:T(8,128)(2,1)S(1)}, bf16[1,2048,192]{1,2,0:T(8,128)(2,1)}, u32[]{:S(2)}) copy-start(bf16[1,2048,192]{1,2,0:T(8,128)(2,1)} %param.20) | copy-start | bytes 2359300
  215.2 9.4 %copy-start.7 = (f32[128,8]{0,1:T(8,128)S(1)}, f32[128,8]{0,1:T(8,128)}, u32[]{:S(2)}) copy-start(f32[128,8]{0,1:T(8,128)} %param.19) | copy-start | bytes 12292
  215.2 113.9 %all-to-all-start.1 = ((bf16[64,12,2048]{2,1,0:T(8,128)(2,1)}), bf16[64,12,2048]{2,1,0:T(8,128)(2,1)}, u32[]{:S(2)}, u32[]{:S(2)}) async-start(bf16[64,12,2048]{2,1,0:T(8,128)(2,1)} %reshape.258), calls=%async_computation.2 | async-start | bytes 8388608 | tf_op jit(solution)/shard_map/all_to_all | solution.py:109
  224.5 198.1 %reduce-scatter.5.cloned.1.call-start = ((), (), s32[]{:S(2)}) async-start(), calls=%async_computation.5 | async-start | bytes 589824 | tf_op jit(solution)/shard_map/reduce_scatter | solution.py:116
  335.8 17.3 %copy-start.5 = (bf16[32,128]{1,0:T(8,128)(2,1)S(1)}, bf16[32,128]{1,0:T(8,128)(2,1)}, u32[]{:S(2)}) copy-start(bf16[32,128]{1,0:T(8,128)(2,1)} %param.25) | copy-start | bytes 24580
  335.8 84.8 %copy-start.9 = (f32[128]{0:T(128)S(1)}, f32[128]{0:T(128)}, u32[]{:S(2)}) copy-start(f32[128]{0:T(128)} %param.26) | copy-start | bytes 1540
  335.8 87.8 %copy-start.6 = (f32[2048]{0:T(1024)S(1)}, f32[2048]{0:T(1024)}, u32[]{:S(2)}) copy-start(f32[2048]{0:T(1024)} %param.23) | copy-start | bytes 24580
  352.5 122.9 %all-gather.2.cloned.1.call-start = ((), (), s32[]{:S(2)}) async-start(), calls=%async_computation.6 | async-start | bytes 2129920 | tf_op jit(solution)/shard_map/all_gather | solution.py:126
  420.7 62.3 %copy-start.8 = (f32[128]{0:T(128)S(1)}, f32[128]{0:T(128)}, u32[]{:S(2)}) copy-start(f32[128]{0:T(128)} %param.27) | copy-start | bytes 1540
  423.6 60.3 %copy-start.1 = (bf16[16,2048]{1,0:T(8,128)(2,1)}, bf16[16,2048]{1,0:T(8,128)(2,1)S(1)}, u32[]{:S(2)}) copy-start(bf16[16,2048]{1,0:T(8,128)(2,1)S(1)} %get-tuple-element.16) | copy-start | bytes 196612
Sparse Core Ops, SparseCore 0:
  12.1 39.1 reduce-scatter.2
  352.6 69.9 reduce-scatter.4
Sparse Core Ops, SparseCore 1:
  356.1 119.3 all-gather.1
